TPU v7x, 32 devices: a whole 2x2x4 slice. The times are simulated.
32 devices in a mesh: dap: 8 (over z, core), ch: 4 (over y, x).
Axes of the slice: x: 2, y: 2, z: 4, core: 2. Of those that a mesh axis runs over, the one named last changes fastest.
Arguments:
- pair_rep: bfloat16 [120, 120, 128], P('dap', 'ch'), may hold values from -400 to 400
- residue_mask: int32 [120], replicated, may hold values 0 or 1
- w_proj: bfloat16 [128, 512], replicated, may hold values from -0.5 to 0.5
- w_gate: bfloat16 [128, 128], replicated, may hold values from -0.5 to 0.5
- w_out: bfloat16 [128, 128], replicated, may hold values from -0.5 to 0.5
- cotangent: bfloat16 [120, 120, 128], P('dap', 'ch'), may hold values from -6 to 6
Outputs:
- pair_update: bfloat16 [120, 120, 128], P('dap', 'ch')
- grad_pair: bfloat16 [120, 120, 128], P('dap', 'ch')
Inputs may be any that keep to these rules, and one draw needn't show every extreme that they name: `residue_mask`: 1 marks a residue of the crop, 0 a padding position.
All inputs are finite; a program needn't handle non-finite values.
Results may differ from a plain program's by a relative error of at most 0.0085.
Values may be sent and summed in bfloat16 or wider, within the bound.
No kernel may reach another device: no remote copies, remote signals or barrier semaphores. Data moves between devices by JAX's collectives and lax.ppermute only.
A program may use at most 64 MiB of HBM per device.

v0:
```python
import jax
import jax.numpy as jnp
from jax import lax
from jax.sharding import PartitionSpec as P

EPSILON = 1e-05


def normalize(values, axis):
    center = jnp.mean(values, axis=axis, keepdims=True)
    spread = values - center
    scale_inv = lax.rsqrt(jnp.mean(spread * spread, axis=axis, keepdims=True) + EPSILON)
    return (spread * scale_inv, scale_inv)


def norm_back(grad_in, normed, scale_inv, axis):
    first = jnp.mean(grad_in, axis=axis, keepdims=True)
    second = jnp.mean(grad_in * normed, axis=axis, keepdims=True)
    return scale_inv * (grad_in - first - normed * second)


def on_device(pair_rep, residue_mask, w_proj, w_gate, w_out, cotangent):
    row_count, columns, channels = pair_rep.shape
    hidden_width = w_out.shape[0]
    row_start = lax.axis_index("dap") * row_count
    col_start = lax.axis_index("ch") * columns
    live_flags = residue_mask.astype(jnp.float32)
    row_live = lax.dynamic_slice_in_dim(live_flags, row_start, row_count, 0)
    col_live = lax.dynamic_slice_in_dim(live_flags, col_start, columns, 0)
    cell_mask = row_live[:, None] * col_live[None, :]
    normed, pair_scale = normalize(pair_rep.astype(jnp.float32), 2)
    normed_half = normed.astype(jnp.bfloat16)
    projected = jnp.einsum("rkd,de->erk", normed_half, w_proj, preferred_element_type=jnp.float32)
    left_sig = jax.nn.sigmoid(projected[:hidden_width])
    left_val = projected[hidden_width : 2 * hidden_width]
    right_sig = jax.nn.sigmoid(projected[2 * hidden_width : 3 * hidden_width])
    right_val = projected[3 * hidden_width :]
    left_cells = (left_sig * left_val * cell_mask).astype(jnp.bfloat16)
    right_cells = (right_sig * right_val * cell_mask).astype(jnp.bfloat16)
    gate_values = jax.nn.sigmoid(
        jnp.einsum("rkd,de->rke", normed_half, w_gate, preferred_element_type=jnp.float32)
    )
    left_rows, right_rows = (
        lax.all_to_all(left_cells, "ch", split_axis=0, concat_axis=2, tiled=True),
        lax.all_to_all(right_cells, "ch", split_axis=0, concat_axis=2, tiled=True),
    )
    product = jnp.einsum(
        "cik,cjk->cij",
        left_rows,
        lax.all_gather(right_rows, "dap", axis=1, tiled=True),
        preferred_element_type=jnp.float32,
    ).astype(jnp.bfloat16)
    product_cells = lax.all_to_all(product, "ch", split_axis=2, concat_axis=0, tiled=True)
    hidden_norm, hidden_scale = normalize(product_cells.astype(jnp.float32), 0)
    hidden_half = hidden_norm.astype(jnp.bfloat16)
    projected_out = jnp.einsum(
        "hrk,hd->rkd", hidden_half, w_out, preferred_element_type=jnp.float32
    )
    pair_update = (gate_values * projected_out).astype(jnp.bfloat16)
    upstream = cotangent.astype(jnp.float32)
    grad_out = (upstream * gate_values).astype(jnp.bfloat16)
    grad_logit = (upstream * projected_out * gate_values * (1.0 - gate_values)).astype(jnp.bfloat16)
    grad_hidden = jnp.einsum("rkd,hd->hrk", grad_out, w_out, preferred_element_type=jnp.float32)
    grad_product = norm_back(grad_hidden, hidden_norm, hidden_scale, 0).astype(jnp.bfloat16)
    grad_rows = lax.all_to_all(grad_product, "ch", split_axis=0, concat_axis=2, tiled=True)
    piece_left = lax.all_gather(left_rows, "dap", axis=1, tiled=True)
    piece_right = lax.all_gather(right_rows, "dap", axis=1, tiled=True)
    piece_grad = lax.all_gather(grad_rows, "dap", axis=1, tiled=True)
    cross_slab = lax.dynamic_slice_in_dim(piece_grad, row_start, row_count, 2)
    new_left = jnp.einsum(
        "cij,cjk->cik", grad_rows, piece_right, preferred_element_type=jnp.float32
    )
    new_right = jnp.einsum(
        "cij,cik->cjk", cross_slab, piece_left, preferred_element_type=jnp.float32
    )
    left_back, right_back = (
        lax.all_to_all(
            new_left.astype(jnp.bfloat16), "ch", split_axis=2, concat_axis=0, tiled=True
        ),
        lax.all_to_all(
            new_right.astype(jnp.bfloat16), "ch", split_axis=2, concat_axis=0, tiled=True
        ),
    )
    masked_left = left_back.astype(jnp.float32) * cell_mask
    masked_right = right_back.astype(jnp.float32) * cell_mask
    grad_proj = jnp.concatenate(
        [
            masked_left * left_val * left_sig * (1.0 - left_sig),
            masked_left * left_sig,
            masked_right * right_val * right_sig * (1.0 - right_sig),
            masked_right * right_sig,
        ],
        axis=0,
    ).astype(jnp.bfloat16)
    grad_normed = jnp.einsum("erk,de->rkd", grad_proj, w_proj, preferred_element_type=jnp.float32)
    grad_normed = grad_normed + jnp.einsum(
        "rke,de->rkd", grad_logit, w_gate, preferred_element_type=jnp.float32
    )
    grad_pair = norm_back(grad_normed, normed, pair_scale, 2).astype(jnp.bfloat16)
    return (pair_update, grad_pair)


def solution(mesh):
    return jax.shard_map(
        on_device,
        mesh=mesh,
        in_specs=(P("dap", "ch", None), P(), P(), P(), P(), P("dap", "ch", None)),
        out_specs=(P("dap", "ch", None), P("dap", "ch", None)),
        check_vma=False,
    )
```

profile of v0, /device:TPU:0, one launch (start us, length us, event | category | flops | bytes accessed | tf_op | source)
XLA Modules:
  0.0 124.0 jit_solution(5858120735575920195)
XLA Ops:
  0.7 1.1 convert_reduce_fusion
  2.1 0.6 copy-done.13
  2.9 0.3 convolution_bitcast_fusion
  3.4 0.5 copy.73
  3.9 1.3 %reshape.95 = bf16[4,2,7200]{2,1,0:T(2,128)(2,1)} reshape(bf16[128,15,30]{2,1,0:T(8,128)(2,1)S(1)} %copy.73) | data formatting | bytes 230400
  5.2 5.2 %all-to-all-start.1 = ((bf16[4,2,7200]{2,1,0:T(2,128)(2,1)}), bf16[4,2,7200]{2,1,0:T(2,128)(2,1)S(1)}, u32[]{:S(2)}, u32[]{:S(2)}) async-start(bf16[4,2,7200]{2,1,0:T(2,128)(2,1)} %reshape.95), calls=%async_computation.1 | async-start | bytes 233472 | tf_op jit(solution)/shard_map/all_to_all | solution.py:45
  10.4 0.5 copy.71
  10.9 1.3 %reshape.97 = bf16[4,2,7200]{2,1,0:T(2,128)(2,1)} reshape(bf16[128,15,30]{2,1,0:T(8,128)(2,1)S(1)} %copy.71) | data formatting | bytes 230400
  12.2 3.2 %all-to-all-done.1 = bf16[4,2,7200]{2,1,0:T(2,128)(2,1)S(1)} async-done(((bf16[4,2,7200]{2,1,0:T(2,128)(2,1)}), bf16[4,2,7200]{2,1,0:T(2,128)(2,1)S(1)}, u32[]{:S(2)}, u32[]{:S(2)}) %all-to-all-start.1) | async-done | bytes 115232 | tf_op jit(solution)/shard_map/all_to_all | solution.py:45
  15.4 3.3 %all-to-all-start = ((bf16[4,2,7200]{2,1,0:T(2,128)(2,1)}), bf16[4,2,7200]{2,1,0:T(2,128)(2,1)S(1)}, u32[]{:S(2)}, u32[]{:S(2)}) async-start(bf16[4,2,7200]{2,1,0:T(2,128)(2,1)} %reshape.97), calls=%async_computation | async-start | bytes 233472 | tf_op jit(solution)/shard_map/all_to_all | solution.py:44
  18.7 0.5 reshape.96
  19.3 0.4 copy.109
  20.0 17.0 %all_gather.10 = bf16[32,120,120]{2,0,1:T(8,128)(2,1)S(1)} all-gather(bf16[32,15,120]{2,0,1:T(8,128)(2,1)S(1)} %all_to_all.67), channel_id=1, replica_groups=mesh['dap'=8,'ch'=4] {'dap'}, dimensions={1}, use_global_device_ids=true | all-gather | bytes 1036800 | tf_op jit(solution)/shard_map/all_gather | solution.py:50
  37.0 0.5 reshape.98
  37.5 0.4 copy.110
  38.2 0.6 convolution_convert_fusion.1
  38.8 0.4 copy.77
  39.3 0.4 reshape.99
  39.7 8.9 %all_to_all.81 = bf16[4,2,7200]{2,1,0:T(2,128)(2,1)S(1)} all-to-all(bf16[4,2,7200]{2,1,0:T(2,128)(2,1)S(1)} %reshape.99), channel_id=1, replica_groups=mesh['dap'=8,'ch'=4] {'ch'}, dimensions={0} | all-to-all | bytes 230400 | tf_op jit(solution)/shard_map/all_to_all | solution.py:53
  48.7 0.5 reshape.100
  49.2 1.0 copy.78
  50.2 1.3 %reshape.89 = f32[32,15,4,30]{3,2,0,1:T(4,128)S(1)} reshape(bf16[32,15,120]{2,0,1:T(8,128)(2,1)} %copy.78) | data formatting | bytes 345600 | tf_op jit(solution)/shard_map/convert_element_type | solution.py:54
  51.7 1.7 %copy.79 = f32[4,32,15,30]{1,0,3,2:T(4,128)} copy(f32[4,32,15,30]{3,0,1,2:T(4,128)S(1)} %bitcast.66) | data formatting | bytes 460800 | tf_op jit(solution)/shard_map/convert_element_type | solution.py:54
  53.5 1.6 %reshape.85 = f32[128,15,30]{0,2,1:T(8,128)S(1)} reshape(f32[4,32,15,30]{1,0,3,2:T(4,128)} %copy.79) | data formatting | bytes 460800 | tf_op jit(solution)/shard_map/convert_element_type | solution.py:54
  55.1 0.3 multiply_reduce_fusion
  55.4 0.4 copy-done.11
  55.8 0.3 fusion.40
  56.1 0.4 copy-done.12
  56.6 1.0 multiply_convert_fusion.5
  57.6 0.4 fusion.56
  58.0 0.3 copy-done.4
  58.3 0.3 multiply_convert_fusion.4
  58.6 0.5 copy.80
  59.1 1.3 %reshape.101 = bf16[4,2,7200]{2,1,0:T(2,128)(2,1)} reshape(bf16[128,15,30]{2,1,0:T(8,128)(2,1)S(1)} %copy.80) | data formatting | bytes 230400
  60.4 3.4 %all-to-all-start.3 = ((bf16[4,2,7200]{2,1,0:T(2,128)(2,1)}), bf16[4,2,7200]{2,1,0:T(2,128)(2,1)S(1)}, u32[]{:S(2)}, u32[]{:S(2)}) async-start(bf16[4,2,7200]{2,1,0:T(2,128)(2,1)} %reshape.101), calls=%async_computation.3 | async-start | bytes 233472 | tf_op jit(solution)/shard_map/all_to_all | solution.py:65
  63.8 16.8 %all_gather.12 = bf16[32,120,120]{2,0,1:T(8,128)(2,1)} all-gather(bf16[32,15,120]{2,0,1:T(8,128)(2,1)S(1)} %copy-done.3), channel_id=1, replica_groups=mesh['dap'=8,'ch'=4] {'dap'}, dimensions={1}, use_global_device_ids=true | all-gather | bytes 1036800 | tf_op jit(solution)/shard_map/all_gather | solution.py:66
  80.6 0.5 reshape.102
  81.2 0.4 copy.108
  81.9 0.6 convolution_convert_fusion
  82.4 16.5 %all_gather.11 = bf16[32,120,120]{2,0,1:T(8,128)(2,1)S(1)} all-gather(bf16[32,15,120]{2,0,1:T(8,128)(2,1)S(1)} %all_to_all.72), channel_id=1, replica_groups=mesh['dap'=8,'ch'=4] {'dap'}, dimensions={1}, use_global_device_ids=true | all-gather | bytes 1036800 | tf_op jit(solution)/shard_map/all_gather | solution.py:68
  98.9 0.4 copy.84
  99.4 1.1 reshape.105
  100.5 4.2 %all-to-all-start.4 = ((bf16[4,2,7200]{2,1,0:T(2,128)(2,1)}), bf16[4,2,7200]{2,1,0:T(2,128)(2,1)S(1)}, u32[]{:S(2)}, u32[]{:S(2)}) async-start(bf16[4,2,7200]{2,1,0:T(2,128)(2,1)} %reshape.105), calls=%async_computation.4 | async-start | bytes 233472 | tf_op jit(solution)/shard_map/all_to_all | solution.py:77
  104.7 0.3 constant_dynamic-slice_fusion
  105.0 0.9 copy-done.8
  105.9 0.7 convolution_convert_fusion.2
  106.6 0.4 copy.89
  107.0 1.1 reshape.103
  108.1 1.5 %all-to-all-done.4 = bf16[4,2,7200]{2,1,0:T(2,128)(2,1)S(1)} async-done(((bf16[4,2,7200]{2,1,0:T(2,128)(2,1)}), bf16[4,2,7200]{2,1,0:T(2,128)(2,1)S(1)}, u32[]{:S(2)}, u32[]{:S(2)}) %all-to-all-start.4) | async-done | bytes 115232 | tf_op jit(solution)/shard_map/all_to_all | solution.py:77
  109.7 3.5 %all-to-all-start.5 = ((bf16[4,2,7200]{2,1,0:T(2,128)(2,1)}), bf16[4,2,7200]{2,1,0:T(2,128)(2,1)S(1)}, u32[]{:S(2)}, u32[]{:S(2)}) async-start(bf16[4,2,7200]{2,1,0:T(2,128)(2,1)} %reshape.103), calls=%async_computation.5 | async-start | bytes 233472 | tf_op jit(solution)/shard_map/all_to_all | solution.py:80
  113.2 0.5 reshape.106
  113.7 0.4 copy.85
  114.1 0.4 reshape.90
  114.5 1.5 %copy.86 = f32[4,32,15,30]{1,0,3,2:T(4,128)S(1)} copy(f32[4,32,15,30]{3,0,1,2:T(4,128)S(1)} %bitcast.67) | data formatting | bytes 460800 | tf_op jit(solution)/shard_map/convert_element_type | solution.py:84
  116.0 0.4 reshape.86
  116.5 1.5 %all-to-all-done.5 = bf16[4,2,7200]{2,1,0:T(2,128)(2,1)S(1)} async-done(((bf16[4,2,7200]{2,1,0:T(2,128)(2,1)}), bf16[4,2,7200]{2,1,0:T(2,128)(2,1)S(1)}, u32[]{:S(2)}, u32[]{:S(2)}) %all-to-all-start.5) | async-done | bytes 115232 | tf_op jit(solution)/shard_map/all_to_all | solution.py:80
  117.9 0.5 reshape.104
  118.4 0.4 copy.90
  118.8 0.4 reshape.91
  119.3 1.5 %copy.91 = f32[4,32,15,30]{1,0,3,2:T(4,128)S(1)} copy(f32[4,32,15,30]{3,0,1,2:T(4,128)S(1)} %bitcast.68) | data formatting | bytes 460800 | tf_op jit(solution)/shard_map/convert_element_type | solution.py:85
  120.8 0.4 reshape.87
  121.8 0.6 copy-done.5
  122.6 0.4 fusion.55
  123.0 1.0 fusion.23
  (43 shorter events, 2.4 us)
Async XLA Ops:
  0.6 2.2 %copy-start = (bf16[128,512]{1,0:T(8,128)(2,1)S(1)}, bf16[128,512]{1,0:T(8,128)(2,1)}, u32[]{:S(2)}) copy-start(bf16[128,512]{1,0:T(8,128)(2,1)} %param.8) | copy-start | bytes 393220
  0.6 1.1 copy-start.1
  2.0 0.7 copy-start.13
  5.2 10.2 %all-to-all-start.1 = ((bf16[4,2,7200]{2,1,0:T(2,128)(2,1)}), bf16[4,2,7200]{2,1,0:T(2,128)(2,1)S(1)}, u32[]{:S(2)}, u32[]{:S(2)}) async-start(bf16[4,2,7200]{2,1,0:T(2,128)(2,1)} %reshape.95), calls=%async_computation.1 | async-start | bytes 233472 | tf_op jit(solution)/shard_map/all_to_all | solution.py:45
  15.4 21.6 %all-to-all-start = ((bf16[4,2,7200]{2,1,0:T(2,128)(2,1)}), bf16[4,2,7200]{2,1,0:T(2,128)(2,1)S(1)}, u32[]{:S(2)}, u32[]{:S(2)}) async-start(bf16[4,2,7200]{2,1,0:T(2,128)(2,1)} %reshape.97), calls=%async_computation | async-start | bytes 233472 | tf_op jit(solution)/shard_map/all_to_all | solution.py:44
  38.2 0.6 copy-start.2
  55.1 0.8 copy-start.11
  55.8 0.8 copy-start.12
  56.6 1.0 copy-start.6
  56.6 1.0 copy-start.9
  57.6 0.7 copy-start.4
  60.4 3.5 %copy-start.3 = (bf16[32,15,120]{2,0,1:T(8,128)(2,1)S(1)}, bf16[32,15,120]{2,0,1:T(8,128)(2,1)}, u32[]{:S(2)}) copy-start(bf16[32,15,120]{2,0,1:T(8,128)(2,1)} %copy-done.2) | copy-start | bytes 345604
  60.4 20.2 %all-to-all-start.3 = ((bf16[4,2,7200]{2,1,0:T(2,128)(2,1)}), bf16[4,2,7200]{2,1,0:T(2,128)(2,1)S(1)}, u32[]{:S(2)}, u32[]{:S(2)}) async-start(bf16[4,2,7200]{2,1,0:T(2,128)(2,1)} %reshape.101), calls=%async_computation.3 | async-start | bytes 233472 | tf_op jit(solution)/shard_map/all_to_all | solution.py:65
  100.5 9.2 %all-to-all-start.4 = ((bf16[4,2,7200]{2,1,0:T(2,128)(2,1)}), bf16[4,2,7200]{2,1,0:T(2,128)(2,1)S(1)}, u32[]{:S(2)}, u32[]{:S(2)}) async-start(bf16[4,2,7200]{2,1,0:T(2,128)(2,1)} %reshape.105), calls=%async_computation.4 | async-start | bytes 233472 | tf_op jit(solution)/shard_map/all_to_all | solution.py:77
  104.7 1.2 copy-start.8
  109.7 8.3 %all-to-all-start.5 = ((bf16[4,2,7200]{2,1,0:T(2,128)(2,1)}), bf16[4,2,7200]{2,1,0:T(2,128)(2,1)S(1)}, u32[]{:S(2)}, u32[]{:S(2)}) async-start(bf16[4,2,7200]{2,1,0:T(2,128)(2,1)} %reshape.103), calls=%async_computation.5 | async-start | bytes 233472 | tf_op jit(solution)/shard_map/all_to_all | solution.py:80
  121.5 0.9 copy-start.5
  121.5 1.1 copy-start.7
  121.5 1.1 copy-start.10
where the time goes:
time: 125 us; the launch traced here: 124 us
  blocking collectives  59.2 us (47%)
  local copies, waits for them, and re-layouts  29.6 us (24%)
  starting transfers between devices  19.7 us (16%)
  waiting for transfers between devices  6.2 us (5%)
  matrix products  4.56 us (4%)
  other arithmetic  3.66 us (3%)
    all_gather x1, blocking collectives, on_device(): lax.all_gather(right_rows, 'dap', axis=1, tiled=True)  17 us
    all_gather x1, blocking collectives, on_device(): piece_left = lax.all_gather(left_rows, 'dap', axis=1, tiled=True)  16.8 us
    all_gather x1, blocking collectives, on_device(): piece_grad = lax.all_gather(grad_rows, 'dap', axis=1, tiled=True)  16.5 us
    unnamed x40, local copies, waits for them, and re-layouts  13.1 us
    all_to_all x1, blocking collectives, on_device(): lax.all_to_all(product, 'ch', split_axis=2, concat_axis=0, tiled=True)  8.94 us
    all_to_all x1, starting transfers between devices, on_device(): lax.all_to_all(right_cells, 'ch', split_axis=0, concat_axis=2, tiled=True)  5.19 us
    convert_element_type x3, local copies, waits for them, and re-layouts, on_device(): hidden_norm, hidden_scale = normalize(product_cells.astype(jnp.float32), 0)  4.68 us
    all_to_all x1, starting transfers between devices, on_device(): lax.all_to_all(new_left.astype(jnp.bfloat16), 'ch', split_axis=2, concat_...  4.21 us
  transfers between devices with their start and end apart: 5, of which 3 were waited for; matrix products, arithmetic and copies ran while one was open for 7% of the time, Pallas kernels for 0%

commit v1 on v0

--- a/solution.py
+++ b/solution.py
@@ -50,7 +50,10 @@
         lax.all_gather(right_rows, "dap", axis=1, tiled=True),
         preferred_element_type=jnp.float32,
     ).astype(jnp.bfloat16)
-    product_cells = lax.all_to_all(product, "ch", split_axis=2, concat_axis=0, tiled=True)
+    product_cells = jnp.concatenate(
+        lax.all_to_all(jnp.stack(jnp.split(product, lax.axis_size("ch"), axis=2)), "ch", 0, 0),
+        axis=0,
+    )
     hidden_norm, hidden_scale = normalize(product_cells.astype(jnp.float32), 0)
     hidden_half = hidden_norm.astype(jnp.bfloat16)
     projected_out = jnp.einsum(

time: 125 us -> 124 us (level)
  local copies, waits for them, and re-layouts: 29.6 us -> 28.2 us
    convert_element_type x3 -> x2, local copies, waits for them, and re-layouts: 4.68 us -> 3.01 us  [on_device(): hidden_norm, hidden_scale = normalize(product_cells.astype(jnp.float32), 0)]
    unnamed x40 -> x36, local copies, waits for them, and re-layouts: 13.1 us -> 14.6 us
where the time goes in v1:
time: 124 us; the launch traced here: 123 us
  blocking collectives  59.4 us (48%)
  local copies, waits for them, and re-layouts  28.2 us (23%)
  starting transfers between devices  20 us (16%)
  waiting for transfers between devices  6.49 us (5%)
  matrix products  4.57 us (4%)
  other arithmetic  3.63 us (3%)
    all_gather x1, blocking collectives, on_device(): lax.all_gather(right_rows, 'dap', axis=1, tiled=True)  17 us
    all_gather x1, blocking collectives, on_device(): piece_left = lax.all_gather(left_rows, 'dap', axis=1, tiled=True)  16.9 us
    all_gather x1, blocking collectives, on_device(): piece_grad = lax.all_gather(grad_rows, 'dap', axis=1, tiled=True)  16.5 us
    unnamed x36, local copies, waits for them, and re-layouts  14.6 us
    all_to_all x1, blocking collectives, on_device(): lax.all_to_all(jnp.stack(jnp.split(product, lax.axis_size('ch'), axis=2))...  8.94 us
    all_to_all x1, starting transfers between devices, on_device(): lax.all_to_all(right_cells, 'ch', split_axis=0, concat_axis=2, tiled=True)  5.19 us
    all_to_all x1, starting transfers between devices, on_device(): lax.all_to_all(new_left.astype(jnp.bfloat16), 'ch', split_axis=2, concat_...  4.22 us
    all_to_all x1, starting transfers between devices, on_device(): lax.all_to_all(new_right.astype(jnp.bfloat16), 'ch', split_axis=2, concat...  3.93 us
  transfers between devices with their start and end apart: 5, of which 3 were waited for; matrix products, arithmetic and copies ran while one was open for 7% of the time, Pallas kernels for 0%

profile of v1, /device:TPU:0, one launch (start us, length us, event | category | flops | bytes accessed | tf_op | source)
XLA Modules:
  0.0 123.3 jit_solution(1814286337090860428)
XLA Ops:
  0.7 1.1 convert_reduce_fusion.1
  2.1 0.6 copy-done.11
  2.9 0.3 convolution_bitcast_fusion
  3.5 0.5 copy.70
  3.9 1.3 %reshape.90 = bf16[4,2,7200]{2,1,0:T(2,128)(2,1)} reshape(bf16[128,15,30]{2,1,0:T(8,128)(2,1)S(1)} %copy.70) | data formatting | bytes 230400
  5.2 5.2 %all-to-all-start.1 = ((bf16[4,2,7200]{2,1,0:T(2,128)(2,1)}), bf16[4,2,7200]{2,1,0:T(2,128)(2,1)S(1)}, u32[]{:S(2)}, u32[]{:S(2)}) async-start(bf16[4,2,7200]{2,1,0:T(2,128)(2,1)} %reshape.90), calls=%async_computation.1 | async-start | bytes 233472 | tf_op jit(solution)/shard_map/all_to_all | solution.py:45
  10.4 0.5 copy.68
  10.9 1.3 %reshape.92 = bf16[4,2,7200]{2,1,0:T(2,128)(2,1)} reshape(bf16[128,15,30]{2,1,0:T(8,128)(2,1)S(1)} %copy.68) | data formatting | bytes 230400
  12.2 3.2 %all-to-all-done.1 = bf16[4,2,7200]{2,1,0:T(2,128)(2,1)S(1)} async-done(((bf16[4,2,7200]{2,1,0:T(2,128)(2,1)}), bf16[4,2,7200]{2,1,0:T(2,128)(2,1)S(1)}, u32[]{:S(2)}, u32[]{:S(2)}) %all-to-all-start.1) | async-done | bytes 115232 | tf_op jit(solution)/shard_map/all_to_all | solution.py:45
  15.4 3.3 %all-to-all-start = ((bf16[4,2,7200]{2,1,0:T(2,128)(2,1)}), bf16[4,2,7200]{2,1,0:T(2,128)(2,1)S(1)}, u32[]{:S(2)}, u32[]{:S(2)}) async-start(bf16[4,2,7200]{2,1,0:T(2,128)(2,1)} %reshape.92), calls=%async_computation | async-start | bytes 233472 | tf_op jit(solution)/shard_map/all_to_all | solution.py:44
  18.7 0.5 reshape.91
  19.3 0.4 copy.106
  19.7 0.3 all_to_all.63
  20.0 17.0 %all_gather.10 = bf16[32,120,120]{2,0,1:T(8,128)(2,1)S(1)} all-gather(bf16[32,15,120]{2,0,1:T(8,128)(2,1)S(1)} %all_to_all.63), channel_id=1, replica_groups=mesh['dap'=8,'ch'=4] {'dap'}, dimensions={1}, use_global_device_ids=true | all-gather | bytes 1036800 | tf_op jit(solution)/shard_map/all_gather | solution.py:50
  37.0 0.5 reshape.93
  37.5 0.4 copy.107
  37.9 0.3 all_to_all.59
  38.2 0.6 convolution_convert_fusion.1
  39.3 0.6 reshape.94
  39.9 8.9 %all_to_all.77 = bf16[4,2,7200]{2,1,0:T(2,128)(2,1)S(1)} all-to-all(bf16[4,2,7200]{2,1,0:T(2,128)(2,1)S(1)} %reshape.94), channel_id=1, replica_groups=mesh['dap'=8,'ch'=4] {'ch'}, dimensions={0} | all-to-all | bytes 230400 | tf_op jit(solution)/shard_map/all_to_all | solution.py:54
  48.9 0.8 reshape.95
  49.8 1.4 %copy.75 = f32[4,32,15,30]{1,0,3,2:T(4,128)} copy(bf16[4,32,15,30]{3,1,2,0:T(8,128)(2,1)S(1)} %bitcast.73) | data formatting | bytes 345600 | tf_op jit(solution)/shard_map/convert_element_type | solution.py:57
  51.2 1.6 %reshape.82 = f32[128,15,30]{0,2,1:T(8,128)S(1)} reshape(f32[4,32,15,30]{1,0,3,2:T(4,128)} %copy.75) | data formatting | bytes 460800 | tf_op jit(solution)/shard_map/convert_element_type | solution.py:57
  53.0 0.6 copy-done.8
  53.5 0.3 fusion.40
  53.9 0.4 copy-done.9
  54.3 1.0 multiply_convert_fusion.5
  55.3 0.4 fusion.56
  55.7 0.3 copy-done.2
  56.0 0.3 multiply_convert_fusion.4
  56.3 0.5 copy.76
  56.8 1.3 %reshape.96 = bf16[4,2,7200]{2,1,0:T(2,128)(2,1)} reshape(bf16[128,15,30]{2,1,0:T(8,128)(2,1)S(1)} %copy.76) | data formatting | bytes 230400
  58.1 3.3 %all-to-all-start.3 = ((bf16[4,2,7200]{2,1,0:T(2,128)(2,1)}), bf16[4,2,7200]{2,1,0:T(2,128)(2,1)S(1)}, u32[]{:S(2)}, u32[]{:S(2)}) async-start(bf16[4,2,7200]{2,1,0:T(2,128)(2,1)} %reshape.96), calls=%async_computation.3 | async-start | bytes 233472 | tf_op jit(solution)/shard_map/all_to_all | solution.py:68
  61.4 16.9 %all_gather.12 = bf16[32,120,120]{2,0,1:T(8,128)(2,1)} all-gather(bf16[32,15,120]{2,0,1:T(8,128)(2,1)S(1)} %all_to_all.59), channel_id=1, replica_groups=mesh['dap'=8,'ch'=4] {'dap'}, dimensions={1}, use_global_device_ids=true | all-gather | bytes 1036800 | tf_op jit(solution)/shard_map/all_gather | solution.py:69
  78.4 0.5 reshape.97
  78.9 0.4 copy.105
  79.3 0.3 all_to_all.68
  79.6 0.6 convolution_convert_fusion
  80.2 16.5 %all_gather.11 = bf16[32,120,120]{2,0,1:T(8,128)(2,1)S(1)} all-gather(bf16[32,15,120]{2,0,1:T(8,128)(2,1)S(1)} %all_to_all.68), channel_id=1, replica_groups=mesh['dap'=8,'ch'=4] {'dap'}, dimensions={1}, use_global_device_ids=true | all-gather | bytes 1036800 | tf_op jit(solution)/shard_map/all_gather | solution.py:71
  96.7 0.4 copy.80
  97.1 1.1 reshape.100
  98.2 4.2 %all-to-all-start.4 = ((bf16[4,2,7200]{2,1,0:T(2,128)(2,1)}), bf16[4,2,7200]{2,1,0:T(2,128)(2,1)S(1)}, u32[]{:S(2)}, u32[]{:S(2)}) async-start(bf16[4,2,7200]{2,1,0:T(2,128)(2,1)} %reshape.100), calls=%async_computation.4 | async-start | bytes 233472 | tf_op jit(solution)/shard_map/all_to_all | solution.py:80
  102.4 0.3 constant_dynamic-slice_fusion
  102.8 0.9 copy-done.6
  103.6 0.7 convolution_convert_fusion.2
  104.4 0.4 copy.85
  104.8 1.1 reshape.98
  105.9 1.5 %all-to-all-done.4 = bf16[4,2,7200]{2,1,0:T(2,128)(2,1)S(1)} async-done(((bf16[4,2,7200]{2,1,0:T(2,128)(2,1)}), bf16[4,2,7200]{2,1,0:T(2,128)(2,1)S(1)}, u32[]{:S(2)}, u32[]{:S(2)}) %all-to-all-start.4) | async-done | bytes 115232 | tf_op jit(solution)/shard_map/all_to_all | solution.py:80
  107.4 3.9 %all-to-all-start.5 = ((bf16[4,2,7200]{2,1,0:T(2,128)(2,1)}), bf16[4,2,7200]{2,1,0:T(2,128)(2,1)}, u32[]{:S(2)}, u32[]{:S(2)}) async-start(bf16[4,2,7200]{2,1,0:T(2,128)(2,1)} %reshape.98), calls=%async_computation.5 | async-start | bytes 233472 | tf_op jit(solution)/shard_map/all_to_all | solution.py:83
  111.4 0.5 reshape.101
  111.8 0.4 copy.81
  112.3 0.4 reshape.85
  112.7 1.5 %copy.82 = f32[4,32,15,30]{1,0,3,2:T(4,128)S(1)} copy(f32[4,32,15,30]{3,0,1,2:T(4,128)S(1)} %bitcast.74) | data formatting | bytes 460800 | tf_op jit(solution)/shard_map/convert_element_type | solution.py:87
  114.2 0.4 reshape.83
  114.6 1.8 %all-to-all-done.5 = bf16[4,2,7200]{2,1,0:T(2,128)(2,1)} async-done(((bf16[4,2,7200]{2,1,0:T(2,128)(2,1)}), bf16[4,2,7200]{2,1,0:T(2,128)(2,1)}, u32[]{:S(2)}, u32[]{:S(2)}) %all-to-all-start.5) | async-done | bytes 115232 | tf_op jit(solution)/shard_map/all_to_all | solution.py:83
  116.4 1.4 %reshape.99 = bf16[120,15,32]{2,1,0:T(8,128)(2,1)S(1)} reshape(bf16[4,2,7200]{2,1,0:T(2,128)(2,1)} %all-to-all-done.5) | data formatting | bytes 230400
  117.8 0.4 copy.86
  118.2 0.4 reshape.86
  118.6 1.5 %copy.87 = f32[4,32,15,30]{1,0,3,2:T(4,128)S(1)} copy(f32[4,32,15,30]{3,0,1,2:T(4,128)S(1)} %bitcast.75) | data formatting | bytes 460800 | tf_op jit(solution)/shard_map/convert_element_type | solution.py:88
  120.1 0.4 reshape.84
  120.9 0.3 fusion.7
  121.2 0.6 copy-done.3
  121.9 0.4 fusion.55
  122.3 1.0 fusion.23
  (39 shorter events, 1.9 us)
Async XLA Ops:
  0.6 2.2 %copy-start = (bf16[128,512]{1,0:T(8,128)(2,1)S(1)}, bf16[128,512]{1,0:T(8,128)(2,1)}, u32[]{:S(2)}) copy-start(bf16[128,512]{1,0:T(8,128)(2,1)} %param.8) | copy-start | bytes 393220
  0.6 1.1 copy-start.1
  2.0 0.7 copy-start.11
  5.2 10.2 %all-to-all-start.1 = ((bf16[4,2,7200]{2,1,0:T(2,128)(2,1)}), bf16[4,2,7200]{2,1,0:T(2,128)(2,1)S(1)}, u32[]{:S(2)}, u32[]{:S(2)}) async-start(bf16[4,2,7200]{2,1,0:T(2,128)(2,1)} %reshape.90), calls=%async_computation.1 | async-start | bytes 233472 | tf_op jit(solution)/shard_map/all_to_all | solution.py:45
  15.4 21.6 %all-to-all-start = ((bf16[4,2,7200]{2,1,0:T(2,128)(2,1)}), bf16[4,2,7200]{2,1,0:T(2,128)(2,1)S(1)}, u32[]{:S(2)}, u32[]{:S(2)}) async-start(bf16[4,2,7200]{2,1,0:T(2,128)(2,1)} %reshape.92), calls=%async_computation | async-start | bytes 233472 | tf_op jit(solution)/shard_map/all_to_all | solution.py:44
  52.8 0.8 copy-start.8
  53.5 0.8 copy-start.9
  54.3 1.0 copy-start.4
  54.3 1.0 copy-start.7
  55.3 0.7 copy-start.2
  58.1 20.3 %all-to-all-start.3 = ((bf16[4,2,7200]{2,1,0:T(2,128)(2,1)}), bf16[4,2,7200]{2,1,0:T(2,128)(2,1)S(1)}, u32[]{:S(2)}, u32[]{:S(2)}) async-start(bf16[4,2,7200]{2,1,0:T(2,128)(2,1)} %reshape.96), calls=%async_computation.3 | async-start | bytes 233472 | tf_op jit(solution)/shard_map/all_to_all | solution.py:68
  98.2 9.2 %all-to-all-start.4 = ((bf16[4,2,7200]{2,1,0:T(2,128)(2,1)}), bf16[4,2,7200]{2,1,0:T(2,128)(2,1)S(1)}, u32[]{:S(2)}, u32[]{:S(2)}) async-start(bf16[4,2,7200]{2,1,0:T(2,128)(2,1)} %reshape.100), calls=%async_computation.4 | async-start | bytes 233472 | tf_op jit(solution)/shard_map/all_to_all | solution.py:80
  102.4 1.2 copy-start.6
  107.4 9.0 %all-to-all-start.5 = ((bf16[4,2,7200]{2,1,0:T(2,128)(2,1)}), bf16[4,2,7200]{2,1,0:T(2,128)(2,1)}, u32[]{:S(2)}, u32[]{:S(2)}) async-start(bf16[4,2,7200]{2,1,0:T(2,128)(2,1)} %reshape.98), calls=%async_computation.5 | async-start | bytes 233472 | tf_op jit(solution)/shard_map/all_to_all | solution.py:83
  120.8 0.9 copy-start.3
  120.8 1.1 copy-start.5
  120.9 1.0 copy-start.10
